TPU v7x, 32 devices: a whole 2x2x4 slice. The times are simulated.
32 devices in a mesh: alpha: 16 (over z, y, x), beta: 2 (over core).
Axes of the slice: x: 2, y: 2, z: 4, core: 2. Of those that a mesh axis runs over, the one named last changes fastest.
Arguments:
- coeffs: bfloat16 [1, 2048, 4096], P(None, 'alpha', 'beta'), may hold values from -6 to 6
- beta_list: int32 [32, 8], P('beta'), may hold values from 0 to 31
- beta_kind: int32 [32, 8], P('beta'), may hold values from 0 to 7
- opp_beta_kind: int32 [32, 8], P('beta'), may hold values from 0 to 7
- alpha_list: int32 [16, 4], replicated, may hold values from 0 to 15, as said below
- alpha_kind: int32 [16, 4], replicated, may hold values from 0 to 7
- opp_list: int32 [16, 3], replicated, may hold values from 0 to 15, as said below
- opp_kind: int32 [16, 3], replicated, may hold values from 0 to 7
- beta_table: bfloat16 [8, 128, 128], replicated, may hold values from -0.1875 to 0.1875
- alpha_table: bfloat16 [8, 128, 128], replicated, may hold values from -0.25 to 0.25
- opp_alpha_table: bfloat16 [8, 128, 128], replicated, may hold values from -0.3125 to 0.3125
- opp_beta_table: bfloat16 [8, 128, 128], replicated, may hold values from -0.1875 to 0.1875
Outputs:
- sigma_out: bfloat16 [1, 2048, 4096], P(None, 'alpha', 'beta')
Inputs may be any that keep to these rules, and one draw needn't show every extreme that they name: `alpha_list`: each entry of row i lies within 3 of i; the entries of a row are distinct. `opp_list`: each entry of row i lies within 3 of i; the entries of a row are distinct.
All inputs are finite; a program needn't handle non-finite values.
Results may differ from a plain program's by a relative error of at most 0.0034.
Values may be sent and summed in bfloat16 or wider, within the bound.
A program may use at most 128 MiB of HBM per device.

v0:
```python
import jax
import jax.numpy as jnp
from jax import lax
from jax.sharding import PartitionSpec as P

REACH = 3


def shifted(block, axis, distance):
    devices = range(lax.axis_size(axis))
    route = [(i - distance, i) for i in devices if i - distance in devices]
    return lax.ppermute(block, axis, route)


def beta_apply(row_data, sources, kind_ids, tile_table):
    root_count, row_count, col_count = row_data.shape
    tile_size = tile_table.shape[1]
    tiled = row_data.reshape(root_count, row_count, col_count // tile_size, tile_size)
    picked = jnp.take(tiled, sources, axis=2)
    tile_sets = jnp.take(tile_table, kind_ids, axis=0)
    summed = jnp.einsum("rajmt,jmst->rajs", picked, tile_sets, preferred_element_type=jnp.float32)
    return summed.reshape(root_count, row_count, -1)


def nearby_sum(stacked, sources, kind_ids, tile_table, own_block):
    summed = jnp.zeros(stacked.shape[1:], jnp.float32)
    for link in range(sources.shape[0]):
        position = sources[link] - own_block + REACH
        picked = lax.dynamic_index_in_dim(stacked, position, 0, keepdims=False)
        tile_one = lax.dynamic_index_in_dim(tile_table, kind_ids[link], 0, keepdims=False)
        summed = summed + jnp.einsum(
            "st,rtc->rsc", tile_one, picked, preferred_element_type=jnp.float32
        )
    return summed


def local(
    coeffs,
    beta_list,
    beta_kind,
    opp_beta_kind,
    alpha_list,
    alpha_kind,
    opp_list,
    opp_kind,
    beta_table,
    alpha_table,
    opp_alpha_table,
    opp_beta_table,
):
    whole_cols = lax.all_gather(coeffs, "beta", axis=2, tiled=True)
    beta_part = beta_apply(whole_cols, beta_list, beta_kind, beta_table)
    own_block = lax.axis_index("alpha")
    nearby = []
    for slot in range(2 * REACH + 1):
        if slot == REACH:
            nearby.append(coeffs)
        else:
            nearby.append(shifted(coeffs, "alpha", REACH - slot))
    stacked = jnp.stack(nearby)
    alpha_part = nearby_sum(
        stacked,
        lax.dynamic_index_in_dim(alpha_list, own_block, 0, keepdims=False),
        lax.dynamic_index_in_dim(alpha_kind, own_block, 0, keepdims=False),
        alpha_table,
        own_block,
    )
    half_sum = nearby_sum(
        stacked,
        lax.dynamic_index_in_dim(opp_list, own_block, 0, keepdims=False),
        lax.dynamic_index_in_dim(opp_kind, own_block, 0, keepdims=False),
        opp_alpha_table,
        own_block,
    ).astype(jnp.bfloat16)
    half_whole = lax.all_gather(half_sum, "beta", axis=2, tiled=True)
    mixed_part = beta_apply(half_whole, beta_list, opp_beta_kind, opp_beta_table)
    return (beta_part + alpha_part + mixed_part).astype(jnp.bfloat16)


def solution(mesh):
    placed = (
        P(None, "alpha", "beta"),
        P("beta", None),
        P("beta", None),
        P("beta", None),
        P(),
        P(),
        P(),
        P(),
        P(),
        P(),
        P(),
        P(),
    )
    return jax.shard_map(
        local, mesh=mesh, in_specs=placed, out_specs=P(None, "alpha", "beta"), check_vma=False
    )
```

profile of v0, /device:TPU:20, one launch (start us, length us, event | category | flops | bytes accessed | tf_op | source)
XLA Modules:
  0.0 117.5 jit_solution(13060676409522643389)
XLA Ops:
  6.5 4.5 %collective-permute-start = (bf16[1,128,2048]{2,1,0:T(8,128)(2,1)}, bf16[1,128,2048]{2,1,0:T(8,128)(2,1)}, u32[]{:S(2)}, u32[]{:S(2)}) collective-permute-start(bf16[1,128,2048]{2,1,0:T(8,128)(2,1)} %param.16), channel_id=1, source_target_pairs={{0,6},{2,8},{4,10},{6,12},{8,14},{10,16},{12,18},{14,20},{16,22},{... | collective-permute-start | bytes 1572872 | tf_op jit(solution)/shard_map/ppermute | solution.py:12
  11.0 3.4 %collective-permute-start.1 = (bf16[1,128,2048]{2,1,0:T(8,128)(2,1)}, bf16[1,128,2048]{2,1,0:T(8,128)(2,1)S(1)}, u32[]{:S(2)}, u32[]{:S(2)}) collective-permute-start(bf16[1,128,2048]{2,1,0:T(8,128)(2,1)} %param.16), channel_id=1, source_target_pairs={{0,4},{2,6},{4,8},{6,10},{8,12},{10,14},{12,16},{14,18},{16,20},{1... | collective-permute-start | bytes 1572872 | tf_op jit(solution)/shard_map/ppermute | solution.py:12
  14.5 1.9 %collective-permute-start.2 = (bf16[1,128,2048]{2,1,0:T(8,128)(2,1)}, bf16[1,128,2048]{2,1,0:T(8,128)(2,1)S(1)}, u32[]{:S(2)}, u32[]{:S(2)}) collective-permute-start(bf16[1,128,2048]{2,1,0:T(8,128)(2,1)} %param.16), channel_id=1, source_target_pairs={{0,2},{2,4},{4,6},{6,8},{8,10},{10,12},{12,14},{14,16},{16,18},{18... | collective-permute-start | bytes 1572872 | tf_op jit(solution)/shard_map/ppermute | solution.py:12
  16.4 4.8 %collective-permute-start.3 = (bf16[1,128,2048]{2,1,0:T(8,128)(2,1)}, bf16[1,128,2048]{2,1,0:T(8,128)(2,1)S(1)}, u32[]{:S(2)}, u32[]{:S(2)}) collective-permute-start(bf16[1,128,2048]{2,1,0:T(8,128)(2,1)} %param.16), channel_id=1, source_target_pairs={{2,0},{4,2},{6,4},{8,6},{10,8},{12,10},{14,12},{16,14},{18,16},{20... | collective-permute-start | bytes 1572872 | tf_op jit(solution)/shard_map/ppermute | solution.py:12
  21.2 3.3 %collective-permute-start.4 = (bf16[1,128,2048]{2,1,0:T(8,128)(2,1)}, bf16[1,128,2048]{2,1,0:T(8,128)(2,1)S(1)}, u32[]{:S(2)}, u32[]{:S(2)}) collective-permute-start(bf16[1,128,2048]{2,1,0:T(8,128)(2,1)} %param.16), channel_id=1, source_target_pairs={{4,0},{6,2},{8,4},{10,6},{12,8},{14,10},{16,12},{18,14},{20,16},{2... | collective-permute-start | bytes 1572872 | tf_op jit(solution)/shard_map/ppermute | solution.py:12
  24.5 2.1 %copy.37 = bf16[1,128,2048]{1,2,0:T(8,128)(2,1)} copy(bf16[1,128,2048]{2,1,0:T(8,128)(2,1)} %param.16) | data formatting | bytes 1048576 | tf_op args[0]
  26.6 0.0 all-gather.3.cloned.1.call-update
  26.6 0.0 all-gather.5.cloned.1.call-start
  26.7 0.8 constant_dynamic-slice_fusion
  27.5 0.6 fusion.64
  28.1 0.6 fusion.63
  28.7 0.7 compare_select_fusion
  29.4 0.1 copy.39
  29.4 0.1 reshape.169
  29.5 0.1 copy.41
  29.6 0.1 reshape.174
  29.7 0.7 compare_select_fusion.2
  30.4 0.1 copy.35
  30.5 0.1 reshape.164
  30.6 0.8 constant_dynamic-slice_fusion.2
  31.4 0.6 fusion.62
  32.0 0.6 fusion.61
  32.6 0.7 compare_and_fusion.2
  33.3 0.7 compare_and_fusion
  47.5 0.1 copy.40
  47.6 0.1 copy.36
  47.7 0.1 copy.34
  49.7 3.0 %gather_fusion.2 = bf16[128,128,128]{2,1,0:T(8,128)(2,1)} fusion(bf16[8,128,128]{2,1,0:T(8,128)(2,1)S(1)} %copy-done, s32[1024]{0:T(1024)S(1)} %pad_clamp_fusion), kind=kCustom, calls=%fused_computation.2.clone | custom fusion | bytes 8389120 | tf_op jit(solution)/shard_map/jit(_take)/gather | solution.py:20
  52.7 3.1 %gather_fusion = bf16[128,128,128]{2,1,0:T(8,128)(2,1)} fusion(bf16[8,128,128]{2,1,0:T(8,128)(2,1)S(1)} %copy-done.1, s32[1024]{0:T(1024)S(1)} %pad_clamp_fusion.2), kind=kCustom, calls=%fused_computation.clone | custom fusion | bytes 8389120 | tf_op jit(solution)/shard_map/jit(_take)/gather | solution.py:20
  58.5 1.9 %collective-permute-start.5 = (bf16[1,128,2048]{2,1,0:T(8,128)(2,1)S(1)}, bf16[1,128,2048]{2,1,0:T(8,128)(2,1)S(1)}, u32[]{:S(2)}, u32[]{:S(2)}) collective-permute-start(bf16[1,128,2048]{2,1,0:T(8,128)(2,1)S(1)} %copy-done.3), channel_id=1, source_target_pairs={{6,0},{8,2},{10,4},{12,6},{14,8},{16,10},{18,12},{20,14},{22,16},{... | collective-permute-start | bytes 1572872 | tf_op jit(solution)/shard_map/ppermute | solution.py:12
  60.4 1.1 bitcast_dynamic-update-slice_fusion.6
  61.7 12.7 %collective-permute-done.5 = bf16[1,128,2048]{2,1,0:T(8,128)(2,1)S(1)} collective-permute-done((bf16[1,128,2048]{2,1,0:T(8,128)(2,1)S(1)}, bf16[1,128,2048]{2,1,0:T(8,128)(2,1)S(1)}, u32[]{:S(2)}, u32[]{:S(2)}) %collective-permute-start.5) | collective-permute-done | bytes 524320 | tf_op jit(solution)/shard_map/ppermute | solution.py:12
  74.5 1.2 %fusion.23 = f32[2048,128]{1,0:T(8,128)S(1)} fusion(bf16[7,1,128,2048]{3,2,1,0:T(8,128)(2,1)S(1)} %bitcast_dynamic-update-slice_fusion, s32[]{:T(128)S(6)} %select_n.84, bf16[8,128,128]{2,1,0:T(8,128)(2,1)} %param.26, s32[]{:T(128)S(6)} %select_n.85), kind=kOutput, calls=%fused_computation.32 | convolution fusion | flops 67108864 | bytes 1605640 | tf_op jit(solution)/shard_map/st,rtc->rsc/dot_general | solution.py:31
  75.7 1.1 convolution_add_fusion.1
  76.9 1.9 %fusion.17 = bf16[1,128,2048]{1,2,0:T(8,128)(2,1)} fusion(f32[2048,128]{1,0:T(8,128)S(1)} %convolution_add_fusion.1, bf16[7,1,128,2048]{3,2,1,0:T(8,128)(2,1)S(1)} %bitcast_dynamic-update-slice_fusion, s32[]{:T(128)S(6)} %select_n.86, bf16[8,128,128]{2,1,0:T(8,128)(2,1)} %param.26, s32[]{:T(128)S(6)} %select_n.87), kind=kOutput, calls=%fused_computation.26 | convolution fusion | flops 67633152 | bytes 2129928 | tf_op jit(solution)/shard_map/st,rtc->rsc/dot_general | solution.py:31
  78.8 1.4 %fusion.28 = f32[2048,128]{1,0:T(8,128)S(1)} fusion(bf16[7,1,128,2048]{3,2,1,0:T(8,128)(2,1)} %copy-done.2, s32[]{:T(128)S(6)} %select_n.76, bf16[8,128,128]{2,1,0:T(8,128)(2,1)S(1)} %copy-done.4, s32[]{:T(128)S(6)} %select_n.77), kind=kOutput, calls=%fused_computation.37 | convolution fusion | flops 67108864 | bytes 1605640 | tf_op jit(solution)/shard_map/st,rtc->rsc/dot_general | solution.py:31
  80.2 1.4 %convolution_add_fusion.4 = f32[2048,128]{1,0:T(8,128)S(1)} fusion(f32[2048,128]{1,0:T(8,128)S(1)} %fusion.28, bf16[7,1,128,2048]{3,2,1,0:T(8,128)(2,1)} %copy-done.2, s32[]{:T(128)S(6)} %select_n.74, bf16[8,128,128]{2,1,0:T(8,128)(2,1)S(1)} %copy-done.4, s32[]{:T(128)S(6)} %select_n.75), kind=kOutput, calls=%fused_computation.21 | convolution fusion | flops 67371008 | bytes 2654216 | tf_op jit(solution)/shard_map/st,rtc->rsc/dot_general | solution.py:31
  81.6 1.4 %convolution_add_fusion.3 = f32[2048,128]{1,0:T(8,128)S(1)} fusion(f32[2048,128]{1,0:T(8,128)S(1)} %convolution_add_fusion.4, bf16[7,1,128,2048]{3,2,1,0:T(8,128)(2,1)} %copy-done.2, s32[]{:T(128)S(6)} %select_n.78, bf16[8,128,128]{2,1,0:T(8,128)(2,1)S(1)} %copy-done.4, s32[]{:T(128)S(6)} %select_n.79), kind=kOutput, calls=%fused_computation.20 | convolution fusion | flops 67371008 | bytes 2654216 | tf_op jit(solution)/shard_map/st,rtc->rsc/dot_general | solution.py:31
  82.9 0.0 all-gather.3.cloned.1.call-done
  83.0 1.6 %copy.38 = bf16[1,128,32,128]{3,1,2,0:T(8,128)(2,1)S(1)} copy(bf16[1,128,32,128]{1,3,2,0:T(8,128)(2,1)} %bitcast.129) | data formatting | bytes 2097152 | tf_op jit(solution)/shard_map/reshape | solution.py:18
  84.6 3.1 %gather_fusion.1 = bf16[128,128,128]{2,1,0:T(8,128)(2,1)} fusion(bf16[128,32,128]{2,0,1:T(8,128)(2,1)S(1)} %bitcast.121, s32[1024]{0:T(1024)S(1)} %pad_clamp_fusion.1), kind=kCustom, calls=%fused_computation.1.clone | custom fusion | bytes 8389120 | tf_op jit(solution)/shard_map/jit(_take)/gather | solution.py:19
  87.7 4.9 %fusion.2 = f32[16,128,128,1]{2,1,3,0:T(8,128)S(1)} fusion(bf16[1,128,16,8,128]{4,1,3,2,0:T(8,128)(2,1)} %bitcast.125, bf16[16,8,128,128]{3,2,1,0:T(8,128)(2,1)} %bitcast.124, pred[16,8]{1,0:T(8,128)(4,1)S(1)} %copy.36, pred[16,8]{1,0:T(8,128)(4,1)S(1)} %copy.34), kind=kOutput, calls=%fused_computation.6 | convolution fusion | flops 541065216 | bytes 9437440 | tf_op jit(solution)/shard_map/rajmt,jmst->rajs/dot_general | solution.py:21
  92.6 0.0 all-gather.5.cloned.1.call-done
  92.6 4.3 %gather_fusion.3 = bf16[128,128,128]{1,2,0:T(8,128)(2,1)} fusion(bf16[128,32,128]{0,2,1:T(8,128)(2,1)} %bitcast.122, s32[1024]{0:T(1024)S(1)} %pad_clamp_fusion.1), kind=kCustom, calls=%fused_computation.3.clone | custom fusion | bytes 8389120 | tf_op jit(solution)/shard_map/jit(_take)/gather | solution.py:19
  96.9 6.4 %copy.44 = bf16[128,128,128]{2,1,0:T(8,128)(2,1)} copy(bf16[128,128,128]{1,2,0:T(8,128)(2,1)} %gather_fusion.3) | data formatting | bytes 8388608 | tf_op jit(solution)/shard_map/jit(_take)/gather | solution.py:19
  103.3 4.9 %fusion = f32[16,128,128,1]{2,1,3,0:T(8,128)S(1)} fusion(bf16[1,128,16,8,128]{4,1,3,2,0:T(8,128)(2,1)} %bitcast.126, bf16[16,8,128,128]{3,2,1,0:T(8,128)(2,1)} %bitcast.123, pred[16,8]{1,0:T(8,128)(4,1)S(1)} %copy.40, pred[16,8]{1,0:T(8,128)(4,1)S(1)} %copy.36), kind=kOutput, calls=%fused_computation.4 | convolution fusion | flops 541065216 | bytes 9437440 | tf_op jit(solution)/shard_map/rajmt,jmst->rajs/dot_general | solution.py:21
  108.2 1.5 %fusion.15 = bf16[1,128,2048]{1,2,0:T(8,128)(2,1)S(1)} fusion(f32[1,128,2048]{1,2,0:T(8,128)S(1)} %bitcast.128, f32[1,128,2048]{1,2,0:T(8,128)S(1)} %bitcast.127, f32[2048,128]{1,0:T(8,128)S(1)} %convolution_add_fusion.3, bf16[7,1,128,2048]{3,2,1,0:T(8,128)(2,1)} %copy-done.2, s32[]{:T(128)S(6)} %select_n.80, bf16[8,128,128]{2,1,0:T(8,128)(2,1)S(1)} %copy-done.4, ...), kind=kOutput, calls=%fused_computation.24 | convolution fusion | flops 68157440 | bytes 4227080 | tf_op jit(solution)/shard_map/st,rtc->rsc/dot_general | solution.py:31
  109.7 1.0 copy.45
  (26 shorter events, 0.3 us)
Async XLA Ops:
  6.5 43.1 %copy-start = (bf16[8,128,128]{2,1,0:T(8,128)(2,1)S(1)}, bf16[8,128,128]{2,1,0:T(8,128)(2,1)}, u32[]{:S(2)}) copy-start(bf16[8,128,128]{2,1,0:T(8,128)(2,1)} %param.27) | copy-start | bytes 786436
  6.5 76.4 %all-gather.3.cloned.1.call-start = ((), (), s32[]{:S(2)}) async-start(), calls=%async_computation | async-start | bytes 1572864 | tf_op jit(solution)/shard_map/all_gather | solution.py:51
  6.5 51.9 %collective-permute-start = (bf16[1,128,2048]{2,1,0:T(8,128)(2,1)}, bf16[1,128,2048]{2,1,0:T(8,128)(2,1)}, u32[]{:S(2)}, u32[]{:S(2)}) collective-permute-start(bf16[1,128,2048]{2,1,0:T(8,128)(2,1)} %param.16), channel_id=1, source_target_pairs={{0,6},{2,8},{4,10},{6,12},{8,14},{10,16},{12,18},{14,20},{16,22},{... | collective-permute-start | bytes 1572872 | tf_op jit(solution)/shard_map/ppermute | solution.py:12
  11.0 50.5 %collective-permute-start.1 = (bf16[1,128,2048]{2,1,0:T(8,128)(2,1)}, bf16[1,128,2048]{2,1,0:T(8,128)(2,1)S(1)}, u32[]{:S(2)}, u32[]{:S(2)}) collective-permute-start(bf16[1,128,2048]{2,1,0:T(8,128)(2,1)} %param.16), channel_id=1, source_target_pairs={{0,4},{2,6},{4,8},{6,10},{8,12},{10,14},{12,16},{14,18},{16,20},{1... | collective-permute-start | bytes 1572872 | tf_op jit(solution)/shard_map/ppermute | solution.py:12
  14.5 47.1 %collective-permute-start.2 = (bf16[1,128,2048]{2,1,0:T(8,128)(2,1)}, bf16[1,128,2048]{2,1,0:T(8,128)(2,1)S(1)}, u32[]{:S(2)}, u32[]{:S(2)}) collective-permute-start(bf16[1,128,2048]{2,1,0:T(8,128)(2,1)} %param.16), channel_id=1, source_target_pairs={{0,2},{2,4},{4,6},{6,8},{8,10},{10,12},{12,14},{14,16},{16,18},{18... | collective-permute-start | bytes 1572872 | tf_op jit(solution)/shard_map/ppermute | solution.py:12
  16.4 45.2 %collective-permute-start.3 = (bf16[1,128,2048]{2,1,0:T(8,128)(2,1)}, bf16[1,128,2048]{2,1,0:T(8,128)(2,1)S(1)}, u32[]{:S(2)}, u32[]{:S(2)}) collective-permute-start(bf16[1,128,2048]{2,1,0:T(8,128)(2,1)} %param.16), channel_id=1, source_target_pairs={{2,0},{4,2},{6,4},{8,6},{10,8},{12,10},{14,12},{16,14},{18,16},{20... | collective-permute-start | bytes 1572872 | tf_op jit(solution)/shard_map/ppermute | solution.py:12
  21.2 40.5 %collective-permute-start.4 = (bf16[1,128,2048]{2,1,0:T(8,128)(2,1)}, bf16[1,128,2048]{2,1,0:T(8,128)(2,1)S(1)}, u32[]{:S(2)}, u32[]{:S(2)}) collective-permute-start(bf16[1,128,2048]{2,1,0:T(8,128)(2,1)} %param.16), channel_id=1, source_target_pairs={{4,0},{6,2},{8,4},{10,6},{12,8},{14,10},{16,12},{18,14},{20,16},{2... | collective-permute-start | bytes 1572872 | tf_op jit(solution)/shard_map/ppermute | solution.py:12
  26.6 66.0 %all-gather.5.cloned.1.call-start = ((), (), s32[]{:S(2)}) async-start(), calls=%async_computation.1 | async-start | bytes 1572864 | tf_op jit(solution)/shard_map/all_gather | solution.py:75
  49.7 3.0 %copy-start.1 = (bf16[8,128,128]{2,1,0:T(8,128)(2,1)S(1)}, bf16[8,128,128]{2,1,0:T(8,128)(2,1)}, u32[]{:S(2)}) copy-start(bf16[8,128,128]{2,1,0:T(8,128)(2,1)} %param.24) | copy-start | bytes 786436
  52.7 5.7 %copy-start.3 = (bf16[1,128,2048]{2,1,0:T(8,128)(2,1)S(1)}, bf16[1,128,2048]{2,1,0:T(8,128)(2,1)}, u32[]{:S(2)}) copy-start(bf16[1,128,2048]{2,1,0:T(8,128)(2,1)} %param.16) | copy-start | bytes 1572868
  58.5 16.0 %collective-permute-start.5 = (bf16[1,128,2048]{2,1,0:T(8,128)(2,1)S(1)}, bf16[1,128,2048]{2,1,0:T(8,128)(2,1)S(1)}, u32[]{:S(2)}, u32[]{:S(2)}) collective-permute-start(bf16[1,128,2048]{2,1,0:T(8,128)(2,1)S(1)} %copy-done.3), channel_id=1, source_target_pairs={{6,0},{8,2},{10,4},{12,6},{14,8},{16,10},{18,12},{20,14},{22,16},{... | collective-permute-start | bytes 1572872 | tf_op jit(solution)/shard_map/ppermute | solution.py:12
  74.5 2.4 %copy-start.2 = (bf16[7,1,128,2048]{3,2,1,0:T(8,128)(2,1)}, bf16[7,1,128,2048]{3,2,1,0:T(8,128)(2,1)S(1)}, u32[]{:S(2)}) copy-start(bf16[7,1,128,2048]{3,2,1,0:T(8,128)(2,1)S(1)} %bitcast_dynamic-update-slice_fusion) | copy-start | bytes 11010052
  74.5 4.3 %copy-start.4 = (bf16[8,128,128]{2,1,0:T(8,128)(2,1)S(1)}, bf16[8,128,128]{2,1,0:T(8,128)(2,1)}, u32[]{:S(2)}) copy-start(bf16[8,128,128]{2,1,0:T(8,128)(2,1)} %param.25) | copy-start | bytes 786436
Sparse Core Ops, SparseCore 0:
  26.7 8.4 all-gather.2
  78.9 8.3 all-gather.4
where the time goes:
time: 119 us; the launch traced here: 118 us
  between operations  31.8 us (27%)
  local copies, waits for them, and re-layouts  30.6 us (26%)
  starting transfers between devices  19.9 us (17%)
  matrix products  19.6 us (16%)
  waiting for transfers between devices  12.8 us (11%)
  other arithmetic  2.83 us (2%)
    ppermute x6, starting transfers between devices, shifted(): return lax.ppermute(block, axis, route)  19.9 us
    gather x3, local copies, waits for them, and re-layouts, beta_apply(): picked = jnp.take(tiled, sources, axis=2)  13.8 us
    ppermute x6, waiting for transfers between devices, shifted(): return lax.ppermute(block, axis, route)  12.7 us
    dot_general x7, matrix products, nearby_sum(): jnp.einsum('st,rtc->rsc', tile_one, picked, preferred_element_type=jnp.fl...  9.83 us
    dot_general x2, matrix products, beta_apply(): jnp.einsum('rajmt,jmst->rajs', picked, tile_sets, preferred_element_type=...  9.77 us
    gather x2, local copies, waits for them, and re-layouts, beta_apply(): tile_sets = jnp.take(tile_table, kind_ids, axis=0)  6.11 us
    unnamed x17, local copies, waits for them, and re-layouts  3.34 us
  transfers between devices with their start and end apart: 8, of which 1 were waited for; matrix products, arithmetic and copies ran while one was open for 30% of the time, Pallas kernels for 0%

commit v1 on v0

v1 whole, which is shorter than its diff:
```python
import functools

import jax
import jax.numpy as jnp
from jax import lax
from jax.experimental import pallas as pl
from jax.experimental.pallas import tpu as pltpu
from jax.sharding import PartitionSpec as P

CHUNKS = 4
GROUP = 4
BF16, F32 = jnp.bfloat16, jnp.float32
LOW, HIGH, DIAG = range(3)


def picked_tile(block, lists, kinds, table, source):
    kind, found = jnp.int32(0), jnp.int32(0)
    for link in range(lists.shape[1]):
        hit = (lists[block, link] == source).astype(jnp.int32)
        kind += hit * kinds[block, link]
        found += hit
    return table[kind].astype(F32) * found.astype(F32)


def kernel(
    group_count,
    beta_list,
    beta_kind,
    opp_beta_kind,
    alpha_list,
    alpha_kind,
    opp_list,
    opp_kind,
    coeffs,
    beta_table,
    alpha_table,
    opp_alpha_table,
    opp_beta_table,
    out,
    plane,
    cross,
    whole,
    half,
    acc,
    tiles,
    own_send,
    plane_recv,
    relay_send,
    z_send,
    cross_recv,
    hop_send,
    pair_sem,
    half_send,
    half_recv,
):
    rows, cols = coeffs.shape
    width = cols // CHUNKS
    tile = beta_table.shape[1]
    per_half = cols // tile
    per_chunk = width // tile
    me, core = lax.axis_index("alpha"), lax.axis_index("beta")
    z, p = me // GROUP, me % GROUP
    x, y = p % 2, p // 2
    places = (p + 1 - 2 * x, p + 2 - 4 * y, 3 - p)
    mates = tuple(z * GROUP + q for q in places)
    steps = (1 - 2 * x, 1 - 2 * y, 1 - 2 * y)
    middle = x + y == 1

    def inside(group):
        return (group >= 0) & (group < group_count)

    has_out = [inside(z + step) for step in steps]
    has_in = [inside(z - step) for step in steps]

    def chip(index):
        return (index, core)

    pair = (me, 1 - core)

    def send(src, dst, send_sem, recv_sem, device):
        return pltpu.make_async_remote_copy(
            src_ref=src,
            dst_ref=dst,
            send_sem=send_sem,
            recv_sem=recv_sem,
            device_id=device,
            device_id_type=pl.DeviceIdType.MESH,
        )

    def columns(c):
        return pl.ds(c * width, width)

    def own_copy(to, c):
        return send(
            coeffs.at[:, columns(c)], plane.at[to, c], own_send.at[to, c], plane_recv.at[to, c], chip(mates[to])
        )

    def relay_copy(c):
        src, to = (LOW, HIGH) if c % 2 == 0 else (HIGH, LOW)
        return send(plane.at[src, c], plane.at[DIAG, c], relay_send.at[c], plane_recv.at[DIAG, c], chip(mates[to]))

    def z_copy(r, c):
        return send(
            plane.at[r, c], cross.at[r, c], z_send.at[r, c], cross_recv.at[r, c], chip(me + GROUP * steps[r])
        )

    def hop_copy(src, c):
        to = HIGH if src == LOW else LOW
        return send(cross.at[src, c], cross.at[DIAG, c], hop_send.at[src, c], cross_recv.at[DIAG, c], chip(mates[to]))

    def half_copy(c):
        part = half.at[pl.ds(core * per_half + c * per_chunk, per_chunk)]
        return send(part, part, half_send.at[c], half_recv.at[c], pair)

    def pair_copy(t):
        part = coeffs.at[:, pl.ds(t * tile, tile)]
        return send(part, whole.at[core * per_half + t], pair_sem.at[0, t], pair_sem.at[1, t], pair)

    barrier = pltpu.get_barrier_semaphore()
    for device in (chip(mates[LOW]), chip(mates[HIGH]), pair):
        pl.semaphore_signal(barrier, inc=1, device_id=device, device_id_type=pl.DeviceIdType.MESH)
    up, down = inside(z + 1), inside(z - 1)
    for there, offset in ((up, GROUP), (down, -GROUP)):

        @pl.when(there)
        def _():
            pl.semaphore_signal(
                barrier, inc=1, device_id=chip(me + offset), device_id_type=pl.DeviceIdType.MESH
            )

    pl.semaphore_wait(barrier, 3 + up.astype(jnp.int32) + down.astype(jnp.int32))

    for c in range(CHUNKS):
        own_copy(LOW, c).start()
        own_copy(HIGH, c).start()
    for t in range(per_half):
        pair_copy(t).start()
    for t in range(per_half):
        whole[core * per_half + t] = coeffs[:, t * tile : (t + 1) * tile]

    for r in range(3):

        @pl.when(jnp.logical_not(has_in[r]))
        def _():
            cross[r] = jnp.zeros_like(cross[r])

    sources = [me, *mates] + [mates[r] - GROUP * steps[r] for r in range(3)]
    for slot, source in enumerate(sources):
        at = pl.ds(slot * tile, tile)
        tiles[:tile, at] = picked_tile(me, alpha_list, alpha_kind, alpha_table, source).astype(BF16)
        tiles[tile:, at] = picked_tile(me, opp_list, opp_kind, opp_alpha_table, source).astype(BF16)

    def product(first, count, blocks):
        return jnp.dot(
            tiles[:, first * tile : (first + count) * tile],
            jnp.concatenate(blocks, axis=0),
            preferred_element_type=F32,
        )

    def beta_apply(data, kinds, table, j):
        left, right = [], []
        for link in range(beta_list.shape[1]):
            source = beta_list[j, link]
            left.append(data[source])
            right.append(table[kinds[j, link]])
        return lax.dot_general(
            jnp.concatenate(left, axis=1),
            jnp.concatenate(right, axis=1),
            (((1,), (1,)), ((), ())),
            preferred_element_type=F32,
        )

    def tile_at(j):
        return pl.ds(pl.multiple_of(j * tile, tile), tile)

    def z_start(r, c):
        there = has_out[r] & middle if r == DIAG else has_out[r]

        @pl.when(there)
        def _():
            z_copy(r, c).start()

    for c in range(CHUNKS):
        own_copy(LOW, c).wait_recv()
        z_start(LOW, c)
        if c % 2 == 0:
            relay_copy(c).start()
        own_copy(HIGH, c).wait_recv()
        z_start(HIGH, c)
        if c % 2 == 1:
            relay_copy(c).start()
        acc[:, columns(c)] = product(0, 3, [coeffs[:, columns(c)], plane[LOW, c], plane[HIGH, c]])

    for t in range(per_half):
        pair_copy(t).wait_recv()

    def cross_wait(r, c):
        @pl.when(has_in[r])
        def _():
            z_copy(r, c).wait_recv()

    def hop_start(src, c):
        @pl.when(has_in[src] & middle & (x == c % 2))
        def _():
            hop_copy(src, c).start()

    for c in range(CHUNKS):
        relay_copy(c).wait_recv()
        z_start(DIAG, c)
        cross_wait(LOW, c)
        hop_start(LOW, c)
        cross_wait(HIGH, c)
        hop_start(HIGH, c)

        @pl.loop(c * per_chunk, (c + 1) * per_chunk)
        def _(j):
            acc[:tile, tile_at(j)] += beta_apply(whole, beta_kind, beta_table, j)

    for c in range(CHUNKS):
        cross_wait(DIAG, c)
        total = acc[:, columns(c)] + product(3, 4, [plane[DIAG, c], cross[LOW, c], cross[HIGH, c], cross[DIAG, c]])
        for t in range(per_chunk):
            part = total[tile:, t * tile : (t + 1) * tile].astype(BF16)
            half[core * per_half + c * per_chunk + t] = part
        acc[:tile, columns(c)] = total[:tile]
        half_copy(c).start()

    for c in range(CHUNKS):
        half_copy(c).wait()

    @pl.loop(0, per_half)
    def _(j):
        out[:, tile_at(j)] = (acc[:tile, tile_at(j)] + beta_apply(half, opp_beta_kind, opp_beta_table, j)).astype(BF16)

    for t in range(per_half):
        pair_copy(t).wait_send()
    for c in range(CHUNKS):
        own_copy(LOW, c).wait_send()
        own_copy(HIGH, c).wait_send()
        relay_copy(c).wait_send()
        for r in range(3):

            @pl.when(has_out[r] & middle if r == DIAG else has_out[r])
            def _():
                z_copy(r, c).wait_send()

        for src in (LOW, HIGH):

            @pl.when(has_in[src] & middle & (x == c % 2))
            def _():
                hop_copy(src, c).wait_send()


def local(group_count, coeffs, *rest):
    lists, tables = rest[:7], rest[7:]
    flat = coeffs.reshape(coeffs.shape[1:])
    rows, cols = flat.shape
    width = cols // CHUNKS
    tile = tables[0].shape[1]
    vmem = pl.BlockSpec(memory_space=pltpu.VMEM)
    smem = pl.BlockSpec(memory_space=pltpu.SMEM)
    dma = pltpu.SemaphoreType.DMA
    sigma = pl.pallas_call(
        functools.partial(kernel, group_count),
        out_shape=jax.ShapeDtypeStruct((rows, cols), BF16),
        in_specs=[smem] * 7 + [vmem] * 5,
        out_specs=vmem,
        scratch_shapes=[
            pltpu.VMEM((3, CHUNKS, rows, width), BF16),
            pltpu.VMEM((3, CHUNKS, rows, width), BF16),
            pltpu.VMEM((2 * cols // tile, rows, tile), BF16),
            pltpu.VMEM((2 * cols // tile, rows, tile), BF16),
            pltpu.VMEM((2 * tile, cols), F32),
            pltpu.VMEM((2 * tile, 7 * tile), BF16),
            dma((2, CHUNKS)),
            dma((3, CHUNKS)),
            dma((CHUNKS,)),
            dma((3, CHUNKS)),
            dma((3, CHUNKS)),
            dma((2, CHUNKS)),
            dma((2, cols // tile)),
            dma((CHUNKS,)),
            dma((CHUNKS,)),
        ],
        compiler_params=pltpu.CompilerParams(
            collective_id=0, has_side_effects=True, vmem_limit_bytes=40 * 1024 * 1024
        ),
    )(*lists, flat, *tables)
    return sigma.reshape(coeffs.shape)


def solution(mesh):
    halves = P("beta", None)
    return jax.shard_map(
        functools.partial(local, mesh.shape["alpha"] // GROUP),
        mesh=mesh,
        in_specs=(P(None, "alpha", "beta"), halves, halves, halves) + (P(),) * 8,
        out_specs=P(None, "alpha", "beta"),
        check_vma=False,
    )
```

time: 119 us -> 50 us (0.42)
  the two profiles are of different devices: /device:TPU:20 before, /device:TPU:13 now
where the time goes in v1:
time: 50 us; the launch traced here: 49.5 us
  Pallas kernels  39.6 us (79%)
  local copies, waits for them, and re-layouts  9.9 us (20%)
    pallas_call x1, Pallas kernels, local(): pl.pallas_call(functools.partial(kernel, group_count), out_shape=jax.Shap...  39.6 us
    unnamed x30, local copies, waits for them, and re-layouts  9.9 us

profile of v1, /device:TPU:13, one launch (start us, length us, event | category | flops | bytes accessed | tf_op | source)
XLA Modules:
  0.0 49.5 jit_solution(15611432197537716088)
XLA Ops:
  0.0 0.0 copy-start.5
  0.0 0.8 %copy.13.beta_list = s32[16,8]{1,0:T(8,128)S(1)} copy(s32[16,8]{0,1:T(8,128)} %param.13) | data formatting | bytes 1024 | tf_op args[1]
  0.8 0.0 copy-done.5
  0.8 0.0 copy-start.6
  0.8 0.1 copy.14.beta_kind
  0.8 0.6 %copy-done.6 = s32[16,8]{0,1:T(8,128)S(1)} copy-done((s32[16,8]{0,1:T(8,128)S(1)}, s32[16,8]{0,1:T(8,128)}, u32[]{:S(2)}) %copy-start.6) | copy-done | bytes 536
  1.5 0.0 copy-start.7
  1.5 0.1 copy.15.opp_beta_kind
  1.5 0.6 %copy-done.7 = s32[16,4]{0,1:T(4,128)S(1)} copy-done((s32[16,4]{0,1:T(4,128)S(1)}, s32[16,4]{0,1:T(4,128)}, u32[]{:S(2)}) %copy-start.7) | copy-done | bytes 280
  2.1 0.0 copy-start.8
  2.1 0.1 copy.16.alpha_list
  2.2 0.6 %copy-done.8 = s32[16,4]{0,1:T(4,128)S(1)} copy-done((s32[16,4]{0,1:T(4,128)S(1)}, s32[16,4]{0,1:T(4,128)}, u32[]{:S(2)}) %copy-start.8) | copy-done | bytes 280
  2.8 0.0 copy-start.9
  2.8 0.1 copy.17.alpha_kind
  2.9 0.6 %copy-done.9 = s32[16,3]{0,1:T(4,128)S(1)} copy-done((s32[16,3]{0,1:T(4,128)S(1)}, s32[16,3]{0,1:T(4,128)}, u32[]{:S(2)}) %copy-start.9) | copy-done | bytes 216
  3.5 0.0 copy-start.10
  3.5 0.1 copy.18.opp_list
  3.6 0.6 %copy-done.10 = s32[16,3]{0,1:T(4,128)S(1)} copy-done((s32[16,3]{0,1:T(4,128)S(1)}, s32[16,3]{0,1:T(4,128)}, u32[]{:S(2)}) %copy-start.10) | copy-done | bytes 216
  4.2 0.1 copy.19.opp_kind
  4.3 0.0 copy-start
  4.3 1.0 %copy-done = bf16[1,128,2048]{2,1,0:T(8,128)(2,1)S(1)} copy-done((bf16[1,128,2048]{2,1,0:T(8,128)(2,1)S(1)}, bf16[1,128,2048]{2,1,0:T(8,128)(2,1)}, u32[]{:S(2)}) %copy-start) | copy-done | bytes 524312
  5.3 0.0 copy-start.1
  5.3 0.9 %copy-done.1 = bf16[8,128,128]{2,1,0:T(8,128)(2,1)S(1)} copy-done((bf16[8,128,128]{2,1,0:T(8,128)(2,1)S(1)}, bf16[8,128,128]{2,1,0:T(8,128)(2,1)}, u32[]{:S(2)}) %copy-start.1) | copy-done | bytes 262168
  6.3 0.0 copy-start.2
  6.3 0.9 %copy-done.2 = bf16[8,128,128]{2,1,0:T(8,128)(2,1)S(1)} copy-done((bf16[8,128,128]{2,1,0:T(8,128)(2,1)S(1)}, bf16[8,128,128]{2,1,0:T(8,128)(2,1)}, u32[]{:S(2)}) %copy-start.2) | copy-done | bytes 262168
  7.2 0.0 copy-start.3
  7.2 0.9 %copy-done.3 = bf16[8,128,128]{2,1,0:T(8,128)(2,1)S(1)} copy-done((bf16[8,128,128]{2,1,0:T(8,128)(2,1)S(1)}, bf16[8,128,128]{2,1,0:T(8,128)(2,1)}, u32[]{:S(2)}) %copy-start.3) | copy-done | bytes 262168
  8.2 0.0 copy-start.4
  8.2 0.9 %copy-done.4 = bf16[8,128,128]{2,1,0:T(8,128)(2,1)S(1)} copy-done((bf16[8,128,128]{2,1,0:T(8,128)(2,1)S(1)}, bf16[8,128,128]{2,1,0:T(8,128)(2,1)}, u32[]{:S(2)}) %copy-start.4) | copy-done | bytes 262168
  9.1 39.6 %shard_map.118 = bf16[128,2048]{1,0:T(8,128)(2,1)S(1)} custom-call(s32[16,8]{1,0:T(8,128)S(1)} %copy.13.beta_list, s32[16,8]{1,0:T(8,128)S(1)} %copy.14.beta_kind, s32[16,8]{1,0:T(8,128)S(1)} %copy.15.opp_beta_kind, s32[16,4]{1,0:T(8,128)S(1)} %copy.16.alpha_list, s32[16,4]{1,0:T(8,128)S(1)} %copy.17.alpha_kind, s32[16,3]{1,0:T(8,128)S(1)} %copy.18.opp_list, ...), custom_call_target="tpu_custom_call" | custom-call | tf_op jit(solution)/shard_map/pallas_call | solution.py:263
  48.7 0.8 %copy.21 = bf16[1,128,2048]{2,1,0:T(8,128)(2,1)} copy(bf16[1,128,2048]{2,1,0:T(8,128)(2,1)S(1)} %bitcast.2) | data formatting | bytes 1048576
Async XLA Ops:
  0.0 0.8 %copy-start.5 = (s32[16,8]{0,1:T(8,128)S(1)}, s32[16,8]{0,1:T(8,128)}, u32[]{:S(2)}) copy-start(s32[16,8]{0,1:T(8,128)} %param.14) | copy-start | bytes 1540
  0.8 0.7 %copy-start.6 = (s32[16,8]{0,1:T(8,128)S(1)}, s32[16,8]{0,1:T(8,128)}, u32[]{:S(2)}) copy-start(s32[16,8]{0,1:T(8,128)} %param.15) | copy-start | bytes 1540
  1.5 0.7 %copy-start.7 = (s32[16,4]{0,1:T(4,128)S(1)}, s32[16,4]{0,1:T(4,128)}, u32[]{:S(2)}) copy-start(s32[16,4]{0,1:T(4,128)} %param.16) | copy-start | bytes 772
  2.1 0.7 %copy-start.8 = (s32[16,4]{0,1:T(4,128)S(1)}, s32[16,4]{0,1:T(4,128)}, u32[]{:S(2)}) copy-start(s32[16,4]{0,1:T(4,128)} %param.17) | copy-start | bytes 772
  2.8 0.7 %copy-start.9 = (s32[16,3]{0,1:T(4,128)S(1)}, s32[16,3]{0,1:T(4,128)}, u32[]{:S(2)}) copy-start(s32[16,3]{0,1:T(4,128)} %param.18) | copy-start | bytes 580
  3.5 0.7 %copy-start.10 = (s32[16,3]{0,1:T(4,128)S(1)}, s32[16,3]{0,1:T(4,128)}, u32[]{:S(2)}) copy-start(s32[16,3]{0,1:T(4,128)} %param.19) | copy-start | bytes 580
  4.3 1.0 %copy-start = (bf16[1,128,2048]{2,1,0:T(8,128)(2,1)S(1)}, bf16[1,128,2048]{2,1,0:T(8,128)(2,1)}, u32[]{:S(2)}) copy-start(bf16[1,128,2048]{2,1,0:T(8,128)(2,1)} %param.12) | copy-start | bytes 1572868
  5.3 0.9 %copy-start.1 = (bf16[8,128,128]{2,1,0:T(8,128)(2,1)S(1)}, bf16[8,128,128]{2,1,0:T(8,128)(2,1)}, u32[]{:S(2)}) copy-start(bf16[8,128,128]{2,1,0:T(8,128)(2,1)} %beta_table.1) | copy-start | bytes 786436
  6.3 0.9 %copy-start.2 = (bf16[8,128,128]{2,1,0:T(8,128)(2,1)S(1)}, bf16[8,128,128]{2,1,0:T(8,128)(2,1)}, u32[]{:S(2)}) copy-start(bf16[8,128,128]{2,1,0:T(8,128)(2,1)} %alpha_table.1) | copy-start | bytes 786436
  7.2 0.9 %copy-start.3 = (bf16[8,128,128]{2,1,0:T(8,128)(2,1)S(1)}, bf16[8,128,128]{2,1,0:T(8,128)(2,1)}, u32[]{:S(2)}) copy-start(bf16[8,128,128]{2,1,0:T(8,128)(2,1)} %opp_alpha_table.1) | copy-start | bytes 786436
  8.2 0.9 %copy-start.4 = (bf16[8,128,128]{2,1,0:T(8,128)(2,1)S(1)}, bf16[8,128,128]{2,1,0:T(8,128)(2,1)}, u32[]{:S(2)}) copy-start(bf16[8,128,128]{2,1,0:T(8,128)(2,1)} %opp_beta_table.1) | copy-start | bytes 786436

commit v2 on v1

--- a/solution.py
+++ b/solution.py
@@ -7,7 +7,7 @@
 from jax.experimental.pallas import tpu as pltpu
 from jax.sharding import PartitionSpec as P
 
-CHUNKS = 4
+CHUNKS = 8
 GROUP = 4
 BF16, F32 = jnp.bfloat16, jnp.float32
 LOW, HIGH, DIAG = range(3)
@@ -15,15 +15,28 @@
 
 def picked_tile(block, lists, kinds, table, source):
     kind, found = jnp.int32(0), jnp.int32(0)
-    for link in range(lists.shape[1]):
-        hit = (lists[block, link] == source).astype(jnp.int32)
-        kind += hit * kinds[block, link]
+    for link in range(lists.shape[0]):
+        hit = (lists[link, block] == source).astype(jnp.int32)
+        kind += hit * kinds[link, block]
         found += hit
     return table[kind].astype(F32) * found.astype(F32)
 
 
 def kernel(
     group_count,
+    beta_list_hbm,
+    beta_kind_hbm,
+    opp_beta_kind_hbm,
+    alpha_list_hbm,
+    alpha_kind_hbm,
+    opp_list_hbm,
+    opp_kind_hbm,
+    coeffs_hbm,
+    beta_table_hbm,
+    alpha_table_hbm,
+    opp_alpha_table_hbm,
+    opp_beta_table_hbm,
+    out,
     beta_list,
     beta_kind,
     opp_beta_kind,
@@ -36,7 +49,7 @@
     alpha_table,
     opp_alpha_table,
     opp_beta_table,
-    out,
+    load_sem,
     plane,
     cross,
     whole,
@@ -92,7 +105,7 @@
 
     def own_copy(to, c):
         return send(
-            coeffs.at[:, columns(c)], plane.at[to, c], own_send.at[to, c], plane_recv.at[to, c], chip(mates[to])
+            coeffs_hbm.at[:, columns(c)], plane.at[to, c], own_send.at[to, c], plane_recv.at[to, c], chip(mates[to])
         )
 
     def relay_copy(c):
@@ -113,8 +126,30 @@
         return send(part, part, half_send.at[c], half_recv.at[c], pair)
 
     def pair_copy(t):
-        part = coeffs.at[:, pl.ds(t * tile, tile)]
+        part = coeffs_hbm.at[:, pl.ds(t * tile, tile)]
         return send(part, whole.at[core * per_half + t], pair_sem.at[0, t], pair_sem.at[1, t], pair)
+
+    loads = [
+        pltpu.make_async_copy(src, dst, load_sem.at[k])
+        for k, (src, dst) in enumerate(
+            (
+                (coeffs_hbm, coeffs),
+                (alpha_list_hbm, alpha_list),
+                (alpha_kind_hbm, alpha_kind),
+                (opp_list_hbm, opp_list),
+                (opp_kind_hbm, opp_kind),
+                (alpha_table_hbm, alpha_table),
+                (opp_alpha_table_hbm, opp_alpha_table),
+                (beta_list_hbm, beta_list),
+                (beta_kind_hbm, beta_kind),
+                (opp_beta_kind_hbm, opp_beta_kind),
+                (beta_table_hbm, beta_table),
+                (opp_beta_table_hbm, opp_beta_table),
+            )
+        )
+    ]
+    for load in loads:
+        load.start()
 
     barrier = pltpu.get_barrier_semaphore()
     for device in (chip(mates[LOW]), chip(mates[HIGH]), pair):
@@ -135,6 +170,8 @@
         own_copy(HIGH, c).start()
     for t in range(per_half):
         pair_copy(t).start()
+    for load in loads:
+        load.wait()
     for t in range(per_half):
         whole[core * per_half + t] = coeffs[:, t * tile : (t + 1) * tile]
 
@@ -159,10 +196,10 @@
 
     def beta_apply(data, kinds, table, j):
         left, right = [], []
-        for link in range(beta_list.shape[1]):
-            source = beta_list[j, link]
+        for link in range(beta_list.shape[0]):
+            source = beta_list[link, j]
             left.append(data[source])
-            right.append(table[kinds[j, link]])
+            right.append(table[kinds[link, j]])
         return lax.dot_general(
             jnp.concatenate(left, axis=1),
             jnp.concatenate(right, axis=1),
@@ -258,14 +295,20 @@
     width = cols // CHUNKS
     tile = tables[0].shape[1]
     vmem = pl.BlockSpec(memory_space=pltpu.VMEM)
-    smem = pl.BlockSpec(memory_space=pltpu.SMEM)
+    hbm = pl.BlockSpec(memory_space=pltpu.HBM)
+    operands = (*(one.T for one in lists), flat, *tables)
+    in_lists = [pltpu.SMEM(one.shape, one.dtype) for one in operands[:7]]
+    in_arrays = [pltpu.VMEM(one.shape, one.dtype) for one in operands[7:]]
     dma = pltpu.SemaphoreType.DMA
     sigma = pl.pallas_call(
         functools.partial(kernel, group_count),
         out_shape=jax.ShapeDtypeStruct((rows, cols), BF16),
-        in_specs=[smem] * 7 + [vmem] * 5,
+        in_specs=[hbm] * len(operands),
         out_specs=vmem,
         scratch_shapes=[
+            *in_lists,
+            *in_arrays,
+            dma((len(operands),)),
             pltpu.VMEM((3, CHUNKS, rows, width), BF16),
             pltpu.VMEM((3, CHUNKS, rows, width), BF16),
             pltpu.VMEM((2 * cols // tile, rows, tile), BF16),
@@ -283,9 +326,9 @@
             dma((CHUNKS,)),
         ],
         compiler_params=pltpu.CompilerParams(
-            collective_id=0, has_side_effects=True, vmem_limit_bytes=40 * 1024 * 1024
+            collective_id=0, has_side_effects=True, vmem_limit_bytes=60 * 1024 * 1024
         ),
-    )(*lists, flat, *tables)
+    )(*operands)
     return sigma.reshape(coeffs.shape)
 
 

time: 50 us -> 40.6 us (0.81)
  local copies, waits for them, and re-layouts: 9.9 us -> 1.88 us
  Pallas kernels: 39.6 us -> 38.3 us
    unnamed x30 -> x1, local copies, waits for them, and re-layouts: 9.9 us -> 1.88 us
    pallas_call x1, Pallas kernels: 39.6 us -> 38.3 us  [local(): pl.pallas_call(functools.partial(kernel, group_count), out_shape=jax.Shap...]
where the time goes in v2:
time: 40.6 us; the launch traced here: 40.2 us
  Pallas kernels  38.3 us (94%)
  local copies, waits for them, and re-layouts  1.88 us (5%)
    pallas_call x1, Pallas kernels, local(): pl.pallas_call(functools.partial(kernel, group_count), out_shape=jax.Shap...  38.3 us
    unnamed x1, local copies, waits for them, and re-layouts  1.88 us

profile of v2, /device:TPU:13, one launch (start us, length us, event | category | flops | bytes accessed | tf_op | source)
XLA Modules:
  0.0 40.2 jit_solution(3448310486710039941)
XLA Ops:
  0.0 38.3 %shard_map.118 = bf16[128,2048]{1,0:T(8,128)(2,1)} custom-call(s32[8,16]{1,0:T(8,128)} %bitcast.11, s32[8,16]{1,0:T(8,128)} %bitcast.12, s32[8,16]{1,0:T(8,128)} %bitcast.13, s32[4,16]{1,0:T(4,128)} %bitcast.14, s32[4,16]{1,0:T(4,128)} %bitcast.15, s32[3,16]{1,0:T(4,128)} %bitcast.16, s32[3,16]{1,0:T(4,128)} %bitcast.17, bf16[128,2048]{1,0:T(8,128)(2,1)} %bitcast.10, ...), custom_call_target="tpu_custom_call" | custom-call | tf_op jit(solution)/shard_map/pallas_call | solution.py:303
  38.3 1.9 %copy.14 = bf16[1,128,2048]{2,1,0:T(8,128)(2,1)} copy(bf16[1,128,2048]{2,1,0:T(8,128)(2,1)} %bitcast.9) | data formatting | bytes 1048576

commit v3 on v2

--- a/solution.py
+++ b/solution.py
@@ -9,6 +9,7 @@
 
 CHUNKS = 8
 GROUP = 4
+UNROLL = 4
 BF16, F32 = jnp.bfloat16, jnp.float32
 LOW, HIGH, DIAG = range(3)
 
@@ -55,6 +56,7 @@
     whole,
     half,
     acc,
+    mine,
     tiles,
     own_send,
     plane_recv,
@@ -217,6 +219,13 @@
         def _():
             z_copy(r, c).start()
 
+    def beta_add(step):
+        span = 2 * per_chunk
+
+        @pl.loop(step * span, (step + 1) * span, unroll=UNROLL)
+        def _(j):
+            mine[:, tile_at(j)] = beta_apply(whole, beta_kind, beta_table, j)
+
     for c in range(CHUNKS):
         own_copy(LOW, c).wait_recv()
         z_start(LOW, c)
@@ -227,12 +236,14 @@
         if c % 2 == 1:
             relay_copy(c).start()
         acc[:, columns(c)] = product(0, 3, [coeffs[:, columns(c)], plane[LOW, c], plane[HIGH, c]])
-
-    for t in range(per_half):
-        pair_copy(t).wait_recv()
-
-    def cross_wait(r, c):
-        @pl.when(has_in[r])
+        if c == CHUNKS // 2 - 1:
+            for t in range(per_half):
+                pair_copy(t).wait_recv()
+        if c >= CHUNKS // 2:
+            beta_add(c - CHUNKS // 2)
+
+    def cross_wait(r, c, there):
+        @pl.when(has_in[r] & there)
         def _():
             z_copy(r, c).wait_recv()
 
@@ -244,30 +255,28 @@
     for c in range(CHUNKS):
         relay_copy(c).wait_recv()
         z_start(DIAG, c)
-        cross_wait(LOW, c)
-        hop_start(LOW, c)
-        cross_wait(HIGH, c)
-        hop_start(HIGH, c)
-
-        @pl.loop(c * per_chunk, (c + 1) * per_chunk)
-        def _(j):
-            acc[:tile, tile_at(j)] += beta_apply(whole, beta_kind, beta_table, j)
-
-    for c in range(CHUNKS):
-        cross_wait(DIAG, c)
+        for r in (LOW, HIGH):
+            cross_wait(r, c, middle)
+            hop_start(r, c)
+
+    for c in range(CHUNKS):
+        cross_wait(LOW, c, jnp.logical_not(middle))
+        cross_wait(HIGH, c, jnp.logical_not(middle))
+        cross_wait(DIAG, c, True)
         total = acc[:, columns(c)] + product(3, 4, [plane[DIAG, c], cross[LOW, c], cross[HIGH, c], cross[DIAG, c]])
         for t in range(per_chunk):
             part = total[tile:, t * tile : (t + 1) * tile].astype(BF16)
             half[core * per_half + c * per_chunk + t] = part
-        acc[:tile, columns(c)] = total[:tile]
+        mine[:, columns(c)] += total[:tile]
         half_copy(c).start()
 
     for c in range(CHUNKS):
         half_copy(c).wait()
 
-    @pl.loop(0, per_half)
+    @pl.loop(0, per_half, unroll=UNROLL)
     def _(j):
-        out[:, tile_at(j)] = (acc[:tile, tile_at(j)] + beta_apply(half, opp_beta_kind, opp_beta_table, j)).astype(BF16)
+        mixed = beta_apply(half, opp_beta_kind, opp_beta_table, j)
+        out[:, tile_at(j)] = (mine[:, tile_at(j)] + mixed).astype(BF16)
 
     for t in range(per_half):
         pair_copy(t).wait_send()
@@ -314,6 +323,7 @@
             pltpu.VMEM((2 * cols // tile, rows, tile), BF16),
             pltpu.VMEM((2 * cols // tile, rows, tile), BF16),
             pltpu.VMEM((2 * tile, cols), F32),
+            pltpu.VMEM((rows, cols), F32),
             pltpu.VMEM((2 * tile, 7 * tile), BF16),
             dma((2, CHUNKS)),
             dma((3, CHUNKS)),

time: 40.6 us -> 38.3 us (0.943)
  Pallas kernels: 38.3 us -> 36.3 us
    pallas_call x1, Pallas kernels: 38.3 us -> 36.3 us  [local(): pl.pallas_call(functools.partial(kernel, group_count), out_shape=jax.Shap...]
where the time goes in v3:
time: 38.3 us; the launch traced here: 38.2 us
  Pallas kernels  36.3 us (95%)
  local copies, waits for them, and re-layouts  1.88 us (5%)
    pallas_call x1, Pallas kernels, local(): pl.pallas_call(functools.partial(kernel, group_count), out_shape=jax.Shap...  36.3 us
    unnamed x1, local copies, waits for them, and re-layouts  1.88 us

profile of v3, /device:TPU:13, one launch (start us, length us, event | category | flops | bytes accessed | tf_op | source)
XLA Modules:
  0.0 38.2 jit_solution(6299877831720108533)
XLA Ops:
  0.0 36.3 %shard_map.118 = bf16[128,2048]{1,0:T(8,128)(2,1)} custom-call(s32[8,16]{1,0:T(8,128)} %bitcast.11, s32[8,16]{1,0:T(8,128)} %bitcast.12, s32[8,16]{1,0:T(8,128)} %bitcast.13, s32[4,16]{1,0:T(4,128)} %bitcast.14, s32[4,16]{1,0:T(4,128)} %bitcast.15, s32[3,16]{1,0:T(4,128)} %bitcast.16, s32[3,16]{1,0:T(4,128)} %bitcast.17, bf16[128,2048]{1,0:T(8,128)(2,1)} %bitcast.10, ...), custom_call_target="tpu_custom_call" | custom-call | tf_op jit(solution)/shard_map/pallas_call | solution.py:312
  36.3 1.9 %copy.14 = bf16[1,128,2048]{2,1,0:T(8,128)(2,1)} copy(bf16[1,128,2048]{2,1,0:T(8,128)(2,1)} %bitcast.9) | data formatting | bytes 1048576

commit v4 on v3

--- a/solution.py
+++ b/solution.py
@@ -57,6 +57,8 @@
     half,
     acc,
     mine,
+    sigma,
+    out_sem,
     tiles,
     own_send,
     plane_recv,
@@ -107,7 +109,7 @@
 
     def own_copy(to, c):
         return send(
-            coeffs_hbm.at[:, columns(c)], plane.at[to, c], own_send.at[to, c], plane_recv.at[to, c], chip(mates[to])
+            coeffs.at[:, columns(c)], plane.at[to, c], own_send.at[to, c], plane_recv.at[to, c], chip(mates[to])
         )
 
     def relay_copy(c):
@@ -167,12 +169,13 @@
 
     pl.semaphore_wait(barrier, 3 + up.astype(jnp.int32) + down.astype(jnp.int32))
 
+    loads[0].wait()
     for c in range(CHUNKS):
         own_copy(LOW, c).start()
         own_copy(HIGH, c).start()
     for t in range(per_half):
         pair_copy(t).start()
-    for load in loads:
+    for load in loads[1:]:
         load.wait()
     for t in range(per_half):
         whole[core * per_half + t] = coeffs[:, t * tile : (t + 1) * tile]
@@ -273,11 +276,19 @@
     for c in range(CHUNKS):
         half_copy(c).wait()
 
-    @pl.loop(0, per_half, unroll=UNROLL)
-    def _(j):
+    def out_copy(k):
+        at = pl.ds(k * UNROLL * tile, UNROLL * tile)
+        return pltpu.make_async_copy(sigma.at[:, at], out.at[:, at], out_sem.at[k])
+
+    for j in range(per_half):
+        at = pl.ds(j * tile, tile)
         mixed = beta_apply(half, opp_beta_kind, opp_beta_table, j)
-        out[:, tile_at(j)] = (mine[:, tile_at(j)] + mixed).astype(BF16)
-
+        sigma[:, at] = (mine[:, at] + mixed).astype(BF16)
+        if j % UNROLL == UNROLL - 1:
+            out_copy(j // UNROLL).start()
+
+    for k in range(per_half // UNROLL):
+        out_copy(k).wait()
     for t in range(per_half):
         pair_copy(t).wait_send()
     for c in range(CHUNKS):
@@ -303,17 +314,16 @@
     rows, cols = flat.shape
     width = cols // CHUNKS
     tile = tables[0].shape[1]
-    vmem = pl.BlockSpec(memory_space=pltpu.VMEM)
     hbm = pl.BlockSpec(memory_space=pltpu.HBM)
     operands = (*(one.T for one in lists), flat, *tables)
     in_lists = [pltpu.SMEM(one.shape, one.dtype) for one in operands[:7]]
     in_arrays = [pltpu.VMEM(one.shape, one.dtype) for one in operands[7:]]
     dma = pltpu.SemaphoreType.DMA
-    sigma = pl.pallas_call(
+    result = pl.pallas_call(
         functools.partial(kernel, group_count),
         out_shape=jax.ShapeDtypeStruct((rows, cols), BF16),
         in_specs=[hbm] * len(operands),
-        out_specs=vmem,
+        out_specs=hbm,
         scratch_shapes=[
             *in_lists,
             *in_arrays,
@@ -324,6 +334,8 @@
             pltpu.VMEM((2 * cols // tile, rows, tile), BF16),
             pltpu.VMEM((2 * tile, cols), F32),
             pltpu.VMEM((rows, cols), F32),
+            pltpu.VMEM((rows, cols), BF16),
+            dma((cols // tile // UNROLL,)),
             pltpu.VMEM((2 * tile, 7 * tile), BF16),
             dma((2, CHUNKS)),
             dma((3, CHUNKS)),
@@ -339,7 +351,7 @@
             collective_id=0, has_side_effects=True, vmem_limit_bytes=60 * 1024 * 1024
         ),
     )(*operands)
-    return sigma.reshape(coeffs.shape)
+    return result.reshape(coeffs.shape)
 
 
 def solution(mesh):

time: 38.3 us -> 37.6 us (0.982)
  Pallas kernels: 36.3 us -> 35.5 us
    pallas_call x1, Pallas kernels: 36.3 us -> 35.5 us  [local(): pl.pallas_call(functools.partial(kernel, group_count), out_shape=jax.Shap...]
where the time goes in v4:
time: 37.6 us; the launch traced here: 37.4 us
  Pallas kernels  35.5 us (94%)
  local copies, waits for them, and re-layouts  1.88 us (5%)
    pallas_call x1, Pallas kernels, local(): pl.pallas_call(functools.partial(kernel, group_count), out_shape=jax.Shap...  35.5 us
    unnamed x1, local copies, waits for them, and re-layouts  1.88 us

profile of v4, /device:TPU:13, one launch (start us, length us, event | category | flops | bytes accessed | tf_op | source)
XLA Modules:
  0.0 37.4 jit_solution(13556116044187928509)
XLA Ops:
  0.0 35.5 %shard_map.118 = bf16[128,2048]{1,0:T(8,128)(2,1)} custom-call(s32[8,16]{1,0:T(8,128)} %bitcast.11, s32[8,16]{1,0:T(8,128)} %bitcast.12, s32[8,16]{1,0:T(8,128)} %bitcast.13, s32[4,16]{1,0:T(4,128)} %bitcast.14, s32[4,16]{1,0:T(4,128)} %bitcast.15, s32[3,16]{1,0:T(4,128)} %bitcast.16, s32[3,16]{1,0:T(4,128)} %bitcast.17, bf16[128,2048]{1,0:T(8,128)(2,1)} %bitcast.10, ...), custom_call_target="tpu_custom_call" | custom-call | tf_op jit(solution)/shard_map/pallas_call | solution.py:322
  35.6 1.9 %copy.14 = bf16[1,128,2048]{2,1,0:T(8,128)(2,1)} copy(bf16[1,128,2048]{2,1,0:T(8,128)(2,1)} %bitcast.9) | data formatting | bytes 1048576
